TPU v7x, 128 devices: a whole 4x4x4 slice. The times are simulated.
128 devices in a mesh: ctx: 16 (over z, y), head: 8 (over x, core).
Axes of the slice: x: 4, y: 4, z: 4, core: 2. Of those that a mesh axis runs over, the one named last changes fastest.
Arguments:
- query_states: bfloat16 [16384, 128, 128], P(('ctx', 'head')), may hold values from -8 to 8
- key_states: bfloat16 [16384, 8, 128], P(('ctx', 'head')), may hold values from -8 to 8
- value_states: bfloat16 [16384, 8, 128], P(('ctx', 'head')), may hold values from -6 to 6
- slash_offsets: int32 [8, 256, 12], P('head'), may hold values from 0 to 31, as said below
- slash_counts: int32 [8, 256], P('head'), may hold values from 1 to 12, as said below
- vertical_blocks: int32 [8, 256, 12], P('head'), may hold values from 0 to 223, as said below
- vertical_counts: int32 [8, 256], P('head'), may hold values from 0 to 12, as said below
Outputs:
- attended: bfloat16 [16384, 128, 128], P(('ctx', 'head'))
Inputs may be any that keep to these rules, and one draw needn't show every extreme that they name: `slash_offsets`: for every head and query block b, the entries j < slash_counts are distinct, at most b and below 32; entry 0 is 0; the other entries are 0. `slash_counts`: at most min(12, b + 1) for query block b. `vertical_blocks`: for every head and query block b, the entries j < vertical_counts are distinct blocks at most b - 32; the other entries are 0. `vertical_counts`: at most max(0, b - 31) for query block b.
All inputs are finite; a program needn't handle non-finite values.
Results may differ from a plain program's by a relative error of at most 0.0049.
Values may be sent and summed in bfloat16 or wider, within the bound.
A program may use at most 128 MiB of HBM per device.

v0:
```python
import jax
import jax.numpy as jnp
from jax import lax
from jax.sharding import PartitionSpec as P

BLK = 64
G = 16
NEG = -1e30


def visit(carry_state, query_group, key_table, value_table, query_ids, blocks, live_slots):
    maxima, totals, running = carry_state
    group_count, block_len, local_groups, group_heads, head_dim = query_group.shape
    head_lanes = jnp.arange(local_groups, dtype=jnp.int32)[None, :, None]
    key_tiles = key_table[blocks, :, head_lanes].reshape(
        group_count, local_groups, 2 * block_len, head_dim
    )
    value_tiles = value_table[blocks, :, head_lanes].reshape(
        group_count, local_groups, 2 * block_len, head_dim
    )
    scores = jnp.einsum(
        "bqngd,bnsd->bngqs", query_group, key_tiles, preferred_element_type=jnp.float32
    ) * head_dim ** (-0.5)
    within = jnp.arange(block_len, dtype=jnp.int32)
    key_pos = (blocks[..., None] * block_len + within).reshape(
        group_count, local_groups, 2 * block_len
    )
    key_live = jnp.repeat(live_slots, block_len, axis=2)
    query_pos = query_ids[:, None] * block_len + within
    visible = key_live[:, :, None, :] & (key_pos[:, :, None, :] <= query_pos[:, None, :, None])
    visible = visible[:, :, None]
    masked = jnp.where(visible, scores, NEG)
    new_max = jnp.maximum(maxima, jnp.max(masked, axis=-1))
    decay_old = jnp.exp(maxima - new_max)
    probs = jnp.where(visible, jnp.exp(scores - new_max[..., None]), 0.0)
    totals = totals * decay_old + jnp.sum(probs, axis=-1)
    running = running * decay_old[..., None] + jnp.einsum(
        "bngqs,bnsd->bngqd",
        probs.astype(jnp.bfloat16),
        value_tiles,
        preferred_element_type=jnp.float32,
    )
    return (new_max, totals, running)


def attend(
    query_group,
    query_ids,
    key_table,
    value_table,
    slash_offsets,
    slash_counts,
    vertical_blocks,
    vertical_counts,
):
    group_count, block_len, local_groups, group_heads, head_dim = query_group.shape
    slash_list = jnp.transpose(slash_offsets[:, query_ids], (1, 0, 2))
    slash_live = jnp.transpose(slash_counts[:, query_ids])
    vertical_list = jnp.transpose(vertical_blocks[:, query_ids], (1, 0, 2))
    vertical_live = jnp.transpose(vertical_counts[:, query_ids])
    state_shape = (group_count, local_groups, group_heads, block_len)
    carry_state = (
        jnp.full(state_shape, NEG, jnp.float32),
        jnp.zeros(state_shape, jnp.float32),
        jnp.zeros(state_shape + (head_dim,), jnp.float32),
    )
    couple = jnp.arange(2, dtype=jnp.int32)

    def slash_step(turn, state_now):
        picked = lax.dynamic_slice_in_dim(slash_list, 2 * turn, 2, axis=2)
        blocks = query_ids[:, None, None] - picked
        live_slots = (2 * turn + couple)[None, None, :] < slash_live[:, :, None]
        return visit(state_now, query_group, key_table, value_table, query_ids, blocks, live_slots)

    def vertical_step(turn, state_now):
        blocks = lax.dynamic_slice_in_dim(vertical_list, 2 * turn, 2, axis=2)
        live_slots = (2 * turn + couple)[None, None, :] < vertical_live[:, :, None]
        return visit(state_now, query_group, key_table, value_table, query_ids, blocks, live_slots)

    carry_state = lax.fori_loop(0, (jnp.max(slash_live) + 1) // 2, slash_step, carry_state)
    carry_state = lax.fori_loop(0, (jnp.max(vertical_live) + 1) // 2, vertical_step, carry_state)
    maxima, totals, running = carry_state
    result = (running / totals[..., None]).astype(jnp.bfloat16)
    return jnp.transpose(result, (0, 3, 1, 2, 4)).reshape(
        group_count * block_len, local_groups * group_heads, head_dim
    )


def on_device(
    query_states,
    key_states,
    value_states,
    slash_offsets,
    slash_counts,
    vertical_blocks,
    vertical_counts,
):
    ctx_rank = lax.axis_index("ctx")
    query_local, key_local, value_local = (
        lax.all_to_all(query_states, "head", split_axis=1, concat_axis=0, tiled=True),
        lax.all_to_all(key_states, "head", split_axis=1, concat_axis=0, tiled=True),
        lax.all_to_all(value_states, "head", split_axis=1, concat_axis=0, tiled=True),
    )
    key_full, value_full = (
        lax.all_gather(key_local, "ctx", axis=0, tiled=True),
        lax.all_gather(value_local, "ctx", axis=0, tiled=True),
    )
    local_rows, heads_local, head_dim = query_local.shape
    local_groups = heads_local // G
    seq_blocks = key_full.shape[0] // BLK
    key_table = key_full.reshape(seq_blocks, BLK, local_groups, head_dim)
    value_table = value_full.reshape(seq_blocks, BLK, local_groups, head_dim)
    query_blocks = local_rows // BLK
    query_ids = ctx_rank * query_blocks + jnp.arange(query_blocks, dtype=jnp.int32)
    group_size = 512 // BLK
    group_total = query_blocks // group_size
    query_grouped = query_local.reshape(group_total, group_size, BLK, local_groups, G, head_dim)

    def run_group(entries):
        return attend(
            entries[0],
            entries[1],
            key_table,
            value_table,
            slash_offsets,
            slash_counts,
            vertical_blocks,
            vertical_counts,
        )

    answers = lax.map(run_group, (query_grouped, query_ids.reshape(group_total, group_size)))
    answers = answers.reshape(local_rows, heads_local, head_dim)
    return lax.all_to_all(answers, "head", split_axis=0, concat_axis=1, tiled=True)


def solution(mesh):
    in_specs = (
        P(("ctx", "head"), None, None),
        P(("ctx", "head"), None, None),
        P(("ctx", "head"), None, None),
        P("head", None, None),
        P("head", None),
        P("head", None, None),
        P("head", None),
    )
    out_specs = P(("ctx", "head"), None, None)
    return jax.shard_map(
        on_device, mesh=mesh, in_specs=in_specs, out_specs=out_specs, check_vma=False
    )
```

profile of v0, /device:TPU:96, one launch (start us, length us, event | category | flops | bytes accessed | tf_op | source)
XLA Modules:
  0.0 660.0 jit_solution(3249853632355213992)
XLA Ops:
  7.5 11.7 %all_to_all.69 = bf16[128,8,128]{2,0,1:T(8,128)(2,1)} all-to-all(bf16[128,8,128]{2,0,1:T(8,128)(2,1)S(1)} %copy.89), channel_id=1, replica_groups=mesh['ctx'=16,'head'=8] {'head'}, dimensions={1} | all-to-all | bytes 524288 | tf_op jit(solution)/shard_map/all_to_all | solution.py:101
  20.3 10.6 %all_to_all.70 = bf16[128,8,128]{2,0,1:T(8,128)(2,1)} all-to-all(bf16[128,8,128]{2,0,1:T(8,128)(2,1)S(1)} %copy.90), channel_id=1, replica_groups=mesh['ctx'=16,'head'=8] {'head'}, dimensions={1} | all-to-all | bytes 524288 | tf_op jit(solution)/shard_map/all_to_all | solution.py:102
  30.9 6.8 %copy.86 = bf16[128,128,128]{2,0,1:T(8,128)(2,1)} copy(bf16[128,128,128]{2,1,0:T(8,128)(2,1)} %param.13) | data formatting | bytes 8388608 | tf_op args[0]
  37.7 4.7 all-to-all-start
  42.7 49.4 %all-to-all-done = bf16[128,128,128]{2,0,1:T(8,128)(2,1)} async-done(((bf16[128,128,128]{2,0,1:T(8,128)(2,1)}), bf16[128,128,128]{2,0,1:T(8,128)(2,1)}, u32[]{:S(2)}, u32[]{:S(2)}) %all-to-all-start) | async-done | bytes 4194336 | tf_op jit(solution)/shard_map/all_to_all | solution.py:100
  92.1 6.9 %copy.88 = bf16[8,128,16,128]{3,2,1,0:T(8,128)(2,1)} copy(bf16[8,128,16,128]{3,1,2,0:T(8,128)(2,1)} %bitcast.17) | data formatting | bytes 8388608 | tf_op jit(solution)/shard_map/all_to_all | solution.py:100
  99.0 24.4 %all-gather.5.cloned.1.call-done = bf16[16384,1,128]{2,0,1:T(8,128)(2,1)} async-done(((bf16[1024,1,128]{2,0,1:T(8,128)(2,1)}), bf16[16384,1,128]{2,0,1:T(8,128)(2,1)}) %all-gather.5.cloned.1.call-update) | async-done | bytes 4194320 | tf_op jit(solution)/shard_map/all_gather | solution.py:106
  123.4 472.6 %while.81 = (s32[]{:T(128)}, bf16[2,512,16,128]{3,2,1,0:T(8,128)(2,1)}, s32[2,8]{1,0:T(2,128)S(1)}, s32[1,256]{1,0:T(1,128)S(1)}, s32[1,256,12]{2,1,0:T(8,128)S(...) while((s32[]{:T(128)}, ...), condition=%wide.region_11.12_spmd, body=%wide.region_0.11_spmd.sunk | while | flops 1103417728 | bytes 111853656 | solution.py:131
  130.9 110.1 %while.82 = (s32[]{:T(128)}, f32[8,1,16,64]{3,2,0,1:T(8,128)S(1)}, f32[8,1,16,64]{3,2,0,1:T(8,128)S(1)}, f32[8,1,16,64,128]{4,3,2,0,1:T(8,128)}, s32[]{:T(128)},...) while((s32[]{:T(128)}, f32[8,1,16,64]{3,2,0,1:T(8,128)S(1)}, ...), condition=%wide.region_5.5_spmd.clone, body=%wide.region_2.4_spmd.clone.sunk | while | flops 550659776 | bytes 42241712 | solution.py:80
  140.7 6.1 bitcast_add_fusion.9
  159.0 6.1 bitcast_add_fusion.9
  171.4 3.1 fusion.75
  177.4 6.1 bitcast_add_fusion.9
  195.7 6.1 bitcast_add_fusion.9
  214.1 6.1 bitcast_add_fusion.9
  226.5 3.1 fusion.75
  232.4 6.1 bitcast_add_fusion.9
  243.6 110.1 %while.83 = (s32[]{:T(128)}, f32[8,1,16,64]{3,2,0,1:T(8,128)S(1)}, f32[8,1,16,64]{3,2,0,1:T(8,128)S(1)}, f32[8,1,16,64,128]{4,3,2,0,1:T(8,128)}, s32[]{:T(128)},...) while((s32[]{:T(128)}, f32[8,1,16,64]{3,2,0,1:T(8,128)S(1)}, ...), condition=%wide.region_10.10_spmd.clone, body=%wide.region_7.9_spmd.clone.sunk | while | flops 550659712 | bytes 42241680 | solution.py:81
  253.4 6.1 bitcast_add_fusion.11
  265.8 3.1 fusion.82
  271.7 6.1 bitcast_add_fusion.11
  290.1 6.1 bitcast_add_fusion.11
  302.5 3.1 fusion.82
  308.4 6.1 bitcast_add_fusion.11
  326.8 6.1 bitcast_add_fusion.11
  339.2 3.1 fusion.82
  345.1 6.1 bitcast_add_fusion.11
  367.2 110.1 %while.82 = (s32[]{:T(128)}, f32[8,1,16,64]{3,2,0,1:T(8,128)S(1)}, f32[8,1,16,64]{3,2,0,1:T(8,128)S(1)}, f32[8,1,16,64,128]{4,3,2,0,1:T(8,128)}, s32[]{:T(128)},...) while((s32[]{:T(128)}, f32[8,1,16,64]{3,2,0,1:T(8,128)S(1)}, ...), condition=%wide.region_5.5_spmd.clone, body=%wide.region_2.4_spmd.clone.sunk | while | flops 550659776 | bytes 42241712 | solution.py:80
  377.0 6.1 bitcast_add_fusion.9
  389.4 3.1 fusion.75
  395.3 6.1 bitcast_add_fusion.9
  413.7 6.1 bitcast_add_fusion.9
  432.0 6.1 bitcast_add_fusion.9
  444.4 3.1 fusion.75
  450.4 6.1 bitcast_add_fusion.9
  468.7 6.1 bitcast_add_fusion.9
  479.9 110.1 %while.83 = (s32[]{:T(128)}, f32[8,1,16,64]{3,2,0,1:T(8,128)S(1)}, f32[8,1,16,64]{3,2,0,1:T(8,128)S(1)}, f32[8,1,16,64,128]{4,3,2,0,1:T(8,128)}, s32[]{:T(128)},...) while((s32[]{:T(128)}, f32[8,1,16,64]{3,2,0,1:T(8,128)S(1)}, ...), condition=%wide.region_10.10_spmd.clone, body=%wide.region_7.9_spmd.clone.sunk | while | flops 550659712 | bytes 42241680 | solution.py:81
  489.7 6.1 bitcast_add_fusion.11
  502.1 3.1 fusion.82
  508.0 6.1 bitcast_add_fusion.11
  526.4 6.1 bitcast_add_fusion.11
  538.8 3.1 fusion.82
  544.7 6.1 bitcast_add_fusion.11
  563.1 6.1 bitcast_add_fusion.11
  575.5 3.1 fusion.82
  581.4 6.1 bitcast_add_fusion.11
  596.0 53.9 %all_to_all.71 = bf16[1024,16,128]{2,1,0:T(8,128)(2,1)S(1)} all-to-all(bf16[1024,16,128]{2,1,0:T(8,128)(2,1)} %bitcast.29), channel_id=1, replica_groups=mesh['ctx'=16,'head'=8] {'head'}, dimensions={0} | all-to-all | bytes 8388608 | tf_op jit(solution)/shard_map/all_to_all | solution.py:133
  649.9 3.3 copy.96
  (695 shorter events, 292.1 us)
Async XLA Ops:
  6.5 92.5 %all-gather.3.cloned.1.call-start = ((), (), s32[]{:S(2)}) async-start(), calls=%async_computation.4 | async-start | bytes 4456448 | tf_op jit(solution)/shard_map/all_gather | solution.py:105
  19.3 104.1 %all-gather.5.cloned.1.call-start = ((), (), s32[]{:S(2)}) async-start(), calls=%async_computation.5 | async-start | bytes 4456448 | tf_op jit(solution)/shard_map/all_gather | solution.py:106
  37.7 4.7 copy-start.4
  37.7 4.9 copy-start.5
  37.7 54.4 %all-to-all-start = ((bf16[128,128,128]{2,0,1:T(8,128)(2,1)}), bf16[128,128,128]{2,0,1:T(8,128)(2,1)}, u32[]{:S(2)}, u32[]{:S(2)}) async-start(bf16[128,128,128]{2,0,1:T(8,128)(2,1)} %copy.86), calls=%async_computation | async-start | bytes 8388608 | tf_op jit(solution)/shard_map/all_to_all | solution.py:100
  92.1 31.3 %copy-start.2 = (s32[1,256]{1,0:T(1,128)S(1)}, s32[1,256]{1,0:T(1,128)}, u32[]{:S(2)}) copy-start(s32[1,256]{1,0:T(1,128)} %param.17) | copy-start | bytes 3076
  92.1 31.3 %copy-start.3 = (s32[1,256]{1,0:T(1,128)S(1)}, s32[1,256]{1,0:T(1,128)}, u32[]{:S(2)}) copy-start(s32[1,256]{1,0:T(1,128)} %param.19) | copy-start | bytes 3076
  140.7 6.1 copy-start
  159.0 6.1 copy-start
  177.4 6.1 copy-start
  195.7 6.1 copy-start
  214.1 6.1 copy-start
  232.4 6.1 copy-start
  253.4 6.1 copy-start.1
  271.7 6.1 copy-start.1
  290.1 6.1 copy-start.1
  308.4 6.1 copy-start.1
  326.8 6.1 copy-start.1
  345.1 6.1 copy-start.1
  376.9 6.1 copy-start
  395.3 6.1 copy-start
  413.7 6.1 copy-start
  432.0 6.1 copy-start
  450.4 6.1 copy-start
  468.7 6.1 copy-start
  489.7 6.1 copy-start.1
  508.0 6.1 copy-start.1
  526.4 6.1 copy-start.1
  544.7 6.1 copy-start.1
  563.1 6.1 copy-start.1
  581.4 6.1 copy-start.1
Sparse Core Ops, SparseCore 0:
  19.4 50.7 all-gather.2
  72.3 51.0 all-gather.4
where the time goes:
time: 662 us; the launch traced here: 660 us
  matrix products  222 us (34%)
  local copies, waits for them, and re-layouts  190 us (29%)
  blocking collectives  76.2 us (12%)
  other arithmetic  74.9 us (11%)
  waiting for transfers between devices  73.8 us (11%)
  between operations  13.4 us (2%)
    dot_general x24, matrix products, visit(): jnp.einsum('bngqs,bnsd->bngqd', probs.astype(jnp.bfloat16), value_tiles,...  147 us
    dot_general x24, matrix products, visit(): jnp.einsum('bqngd,bnsd->bngqs', query_group, key_tiles, preferred_element...  75.1 us
    gather x24, local copies, waits for them, and re-layouts, visit(): key_table[blocks, :, head_lanes]  66.9 us
    gather x24, local copies, waits for them, and re-layouts, visit(): value_table[blocks, :, head_lanes]  66.9 us
    reduce_sum x24, other arithmetic, visit(): totals = totals * decay_old + jnp.sum(probs, axis=-1)  57.2 us
    all_to_all x1, blocking collectives, on_device(): lax.all_to_all(answers, 'head', split_axis=0, concat_axis=1, tiled=True)  53.9 us
    all_to_all x1, waiting for transfers between devices, on_device(): lax.all_to_all(query_states, 'head', split_axis=1, concat_axis=0, tiled=T...  49.4 us
    all_gather x1, waiting for transfers between devices, on_device(): lax.all_gather(value_local, 'ctx', axis=0, tiled=True)  24.4 us
  transfers between devices with their start and end apart: 3, of which 2 were waited for; matrix products, arithmetic and copies ran while one was open for 2% of the time, Pallas kernels for 0%

commit v1 on v0

--- a/solution.py
+++ b/solution.py
@@ -101,9 +101,18 @@
         lax.all_to_all(key_states, "head", split_axis=1, concat_axis=0, tiled=True),
         lax.all_to_all(value_states, "head", split_axis=1, concat_axis=0, tiled=True),
     )
+    ticks_clear = lambda m: jnp.concatenate(
+        jax.lax.all_to_all(
+            jnp.stack([m for _ in range(jax.lax.axis_size("ctx"))]),
+            axis_name="ctx",
+            split_axis=0,
+            concat_axis=0,
+        ),
+        0,
+    )
     key_full, value_full = (
         lax.all_gather(key_local, "ctx", axis=0, tiled=True),
-        lax.all_gather(value_local, "ctx", axis=0, tiled=True),
+        ticks_clear(value_local),
     )
     local_rows, heads_local, head_dim = query_local.shape
     local_groups = heads_local // G

time: 662 us -> 696 us (1.051)
  blocking collectives: 76.2 us -> 119 us
  waiting for transfers between devices: 73.8 us -> 54.6 us
    all_to_all x1, blocking collectives: 10.6 us -> 54.2 us  [on_device(): lax.all_to_all(query_states, 'head', split_axis=1, concat_axis=0, tiled=T...]
    all_gather x1 -> x0, waiting for transfers between devices: 24.4 us -> none  [on_device(): lax.all_gather(value_local, 'ctx', axis=0, tiled=True)]
    all_to_all x1 -> x2, waiting for transfers between devices: 49.4 us -> 54.6 us  [the longest x1 54.1 us: on_device(): jax.lax.all_to_all(jnp.stack([m for _ in range(jax.lax.axis_size('ctx'))]...]
  transfers between devices with their start and end apart: 3 -> 3, of which waited for: 2 -> 2; matrix products, arithmetic and copies ran while one was open for 2% -> 3% of each run, Pallas kernels for 0% -> 0%
where the time goes in v1:
time: 696 us; the launch traced here: 693 us
  matrix products  222 us (32%)
  local copies, waits for them, and re-layouts  194 us (28%)
  blocking collectives  119 us (17%)
  other arithmetic  75 us (11%)
  waiting for transfers between devices  54.6 us (8%)
  between operations  13.4 us (2%)
  starting transfers between devices  10.7 us (2%)
    dot_general x24, matrix products, visit(): jnp.einsum('bngqs,bnsd->bngqd', probs.astype(jnp.bfloat16), value_tiles,...  146 us
    dot_general x24, matrix products, visit(): jnp.einsum('bqngd,bnsd->bngqs', query_group, key_tiles, preferred_element...  75.2 us
    gather x24, local copies, waits for them, and re-layouts, visit(): key_table[blocks, :, head_lanes]  66.9 us
    gather x24, local copies, waits for them, and re-layouts, visit(): value_table[blocks, :, head_lanes]  66.9 us
    reduce_sum x24, other arithmetic, visit(): totals = totals * decay_old + jnp.sum(probs, axis=-1)  57.2 us
    all_to_all x1, blocking collectives, on_device(): lax.all_to_all(query_states, 'head', split_axis=1, concat_axis=0, tiled=T...  54.2 us
    all_to_all x1, waiting for transfers between devices, on_device(): jax.lax.all_to_all(jnp.stack([m for _ in range(jax.lax.axis_size('ctx'))]...  54.1 us
    all_to_all x1, blocking collectives, on_device(): lax.all_to_all(answers, 'head', split_axis=0, concat_axis=1, tiled=True)  53.3 us
  transfers between devices with their start and end apart: 3, of which 2 were waited for; matrix products, arithmetic and copies ran while one was open for 3% of the time, Pallas kernels for 0%

profile of v1, /device:TPU:96, one launch (start us, length us, event | category | flops | bytes accessed | tf_op | source)
XLA Modules:
  0.0 693.4 jit_solution(9896173245592337633)
XLA Ops:
  7.5 11.7 %all_to_all.71 = bf16[128,8,128]{2,0,1:T(8,128)(2,1)} all-to-all(bf16[128,8,128]{2,0,1:T(8,128)(2,1)S(1)} %copy.89), channel_id=1, replica_groups=mesh['ctx'=16,'head'=8] {'head'}, dimensions={1} | all-to-all | bytes 524288 | tf_op jit(solution)/shard_map/all_to_all | solution.py:101
  20.9 3.4 all-to-all-start.2
  24.4 6.9 copy.86
  31.8 54.2 %all_to_all.72 = bf16[128,128,128]{2,0,1:T(8,128)(2,1)} all-to-all(bf16[128,128,128]{2,0,1:T(8,128)(2,1)} %copy.86), channel_id=1, replica_groups=mesh['ctx'=16,'head'=8] {'head'}, dimensions={1} | all-to-all | bytes 8388608 | tf_op jit(solution)/shard_map/all_to_all | solution.py:100
  88.7 7.3 %all-to-all-start.3 = ((bf16[16,1024,1,128]{3,1,2,0:T(8,128)(2,1)}), bf16[16,1024,1,128]{3,1,2,0:T(8,128)(2,1)}, u32[]{:S(2)}, u32[]{:S(2)}) async-start(bf16[16,1024,1,128]{3,1,2,0:T(8,128)(2,1)} %stack.5), calls=%async_computation.3 | async-start | bytes 8388608 | tf_op jit(solution)/shard_map/all_to_all | solution.py:105
  96.3 6.8 copy.88
  103.1 54.1 %all-to-all-done.3 = bf16[16,1024,1,128]{3,1,2,0:T(8,128)(2,1)} async-done(((bf16[16,1024,1,128]{3,1,2,0:T(8,128)(2,1)}), bf16[16,1024,1,128]{3,1,2,0:T(8,128)(2,1)}, u32[]{:S(2)}, u32[]{:S(2)}) %all-to-all-start.3) | async-done | bytes 4194336 | tf_op jit(solution)/shard_map/all_to_all | solution.py:105
  157.2 472.8 %while.81 = (s32[]{:T(128)}, bf16[2,512,16,128]{3,2,1,0:T(8,128)(2,1)}, s32[2,8]{1,0:T(2,128)S(1)}, s32[1,256]{1,0:T(1,128)S(1)}, s32[1,256,12]{2,1,0:T(8,128)S(...) while((s32[]{:T(128)}, ...), condition=%wide.region_11.12_spmd, body=%wide.region_0.11_spmd.sunk | while | flops 1103417728 | bytes 111853656 | solution.py:140
  165.0 110.1 %while.82 = (s32[]{:T(128)}, f32[8,1,16,64]{3,2,0,1:T(8,128)S(1)}, f32[8,1,16,64]{3,2,0,1:T(8,128)S(1)}, f32[8,1,16,64,128]{4,3,2,0,1:T(8,128)}, s32[]{:T(128)},...) while((s32[]{:T(128)}, f32[8,1,16,64]{3,2,0,1:T(8,128)S(1)}, ...), condition=%wide.region_5.5_spmd.clone, body=%wide.region_2.4_spmd.clone.sunk | while | flops 550659776 | bytes 42241712 | solution.py:80
  174.8 6.1 bitcast_add_fusion.9
  187.2 3.1 fusion.75
  193.2 6.1 bitcast_add_fusion.9
  211.5 6.1 bitcast_add_fusion.9
  223.9 3.1 fusion.75
  229.9 6.1 bitcast_add_fusion.9
  242.3 3.1 fusion.75
  248.2 6.1 bitcast_add_fusion.9
  266.6 6.1 bitcast_add_fusion.9
  277.7 110.0 %while.83 = (s32[]{:T(128)}, f32[8,1,16,64]{3,2,0,1:T(8,128)S(1)}, f32[8,1,16,64]{3,2,0,1:T(8,128)S(1)}, f32[8,1,16,64,128]{4,3,2,0,1:T(8,128)}, s32[]{:T(128)},...) while((s32[]{:T(128)}, f32[8,1,16,64]{3,2,0,1:T(8,128)S(1)}, ...), condition=%wide.region_10.10_spmd.clone, body=%wide.region_7.9_spmd.clone.sunk | while | flops 550659712 | bytes 42241680 | solution.py:81
  287.5 6.1 bitcast_add_fusion.11
  299.9 3.1 fusion.82
  305.8 6.1 bitcast_add_fusion.11
  324.2 6.1 bitcast_add_fusion.11
  336.6 3.1 fusion.82
  342.5 6.1 bitcast_add_fusion.11
  360.9 6.1 bitcast_add_fusion.11
  373.3 3.1 fusion.82
  379.2 6.1 bitcast_add_fusion.11
  401.3 110.1 %while.82 = (s32[]{:T(128)}, f32[8,1,16,64]{3,2,0,1:T(8,128)S(1)}, f32[8,1,16,64]{3,2,0,1:T(8,128)S(1)}, f32[8,1,16,64,128]{4,3,2,0,1:T(8,128)}, s32[]{:T(128)},...) while((s32[]{:T(128)}, f32[8,1,16,64]{3,2,0,1:T(8,128)S(1)}, ...), condition=%wide.region_5.5_spmd.clone, body=%wide.region_2.4_spmd.clone.sunk | while | flops 550659776 | bytes 42241712 | solution.py:80
  411.1 6.1 bitcast_add_fusion.9
  429.5 6.1 bitcast_add_fusion.9
  441.9 3.1 fusion.75
  447.8 6.1 bitcast_add_fusion.9
  466.2 6.1 bitcast_add_fusion.9
  478.6 3.1 fusion.75
  484.5 6.1 bitcast_add_fusion.9
  496.9 3.1 fusion.75
  502.9 6.1 bitcast_add_fusion.9
  514.0 110.0 %while.83 = (s32[]{:T(128)}, f32[8,1,16,64]{3,2,0,1:T(8,128)S(1)}, f32[8,1,16,64]{3,2,0,1:T(8,128)S(1)}, f32[8,1,16,64,128]{4,3,2,0,1:T(8,128)}, s32[]{:T(128)},...) while((s32[]{:T(128)}, f32[8,1,16,64]{3,2,0,1:T(8,128)S(1)}, ...), condition=%wide.region_10.10_spmd.clone, body=%wide.region_7.9_spmd.clone.sunk | while | flops 550659712 | bytes 42241680 | solution.py:81
  523.8 6.1 bitcast_add_fusion.11
  542.1 6.1 bitcast_add_fusion.11
  560.5 6.1 bitcast_add_fusion.11
  578.8 6.1 bitcast_add_fusion.11
  591.2 3.1 fusion.82
  597.2 6.1 bitcast_add_fusion.11
  615.5 6.1 bitcast_add_fusion.11
  630.1 53.3 %all_to_all.73 = bf16[1024,16,128]{2,1,0:T(8,128)(2,1)S(1)} all-to-all(bf16[1024,16,128]{2,1,0:T(8,128)(2,1)} %bitcast.29), channel_id=1, replica_groups=mesh['ctx'=16,'head'=8] {'head'}, dimensions={0} | all-to-all | bytes 8388608 | tf_op jit(solution)/shard_map/all_to_all | solution.py:142
  683.3 3.3 copy.96
  (695 shorter events, 296.1 us)
Async XLA Ops:
  6.5 150.7 %all-gather.2.cloned.1.call-start = ((), (), s32[]{:S(2)}) async-start(), calls=%async_computation.5 | async-start | bytes 4456448 | tf_op jit(solution)/shard_map/all_gather | solution.py:114
  20.9 10.8 %all-to-all-start.2 = ((bf16[128,8,128]{2,0,1:T(8,128)(2,1)}), bf16[128,8,128]{2,0,1:T(8,128)(2,1)S(1)}, u32[]{:S(2)}, u32[]{:S(2)}) async-start(bf16[128,8,128]{2,0,1:T(8,128)(2,1)} %copy.90), calls=%async_computation.2 | async-start | bytes 524288 | tf_op jit(solution)/shard_map/all_to_all | solution.py:102
  88.7 7.3 %copy-start.4 = (s32[1,256,12]{1,0,2:T(1,128)S(1)}, s32[1,256,12]{1,0,2:T(1,128)}, u32[]{:S(2)}) copy-start(s32[1,256,12]{1,0,2:T(1,128)} %param.16) | copy-start | bytes 36868
  88.7 7.4 %copy-start.5 = (s32[1,256,12]{1,0,2:T(1,128)S(1)}, s32[1,256,12]{1,0,2:T(1,128)}, u32[]{:S(2)}) copy-start(s32[1,256,12]{1,0,2:T(1,128)} %param.18) | copy-start | bytes 36868
  88.7 68.5 %all-to-all-start.3 = ((bf16[16,1024,1,128]{3,1,2,0:T(8,128)(2,1)}), bf16[16,1024,1,128]{3,1,2,0:T(8,128)(2,1)}, u32[]{:S(2)}, u32[]{:S(2)}) async-start(bf16[16,1024,1,128]{3,1,2,0:T(8,128)(2,1)} %stack.5), calls=%async_computation.3 | async-start | bytes 8388608 | tf_op jit(solution)/shard_map/all_to_all | solution.py:105
  96.3 61.0 %copy-start.2 = (s32[1,256]{1,0:T(1,128)S(1)}, s32[1,256]{1,0:T(1,128)}, u32[]{:S(2)}) copy-start(s32[1,256]{1,0:T(1,128)} %param.17) | copy-start | bytes 3076
  96.3 61.0 %copy-start.3 = (s32[1,256]{1,0:T(1,128)S(1)}, s32[1,256]{1,0:T(1,128)}, u32[]{:S(2)}) copy-start(s32[1,256]{1,0:T(1,128)} %param.19) | copy-start | bytes 3076
  174.8 6.1 copy-start
  193.2 6.1 copy-start
  211.5 6.1 copy-start
  229.9 6.1 copy-start
  248.2 6.1 copy-start
  266.6 6.1 copy-start
  287.5 6.1 copy-start.1
  305.8 6.1 copy-start.1
  324.2 6.1 copy-start.1
  342.5 6.1 copy-start.1
  360.9 6.1 copy-start.1
  379.2 6.1 copy-start.1
  411.1 6.1 copy-start
  429.5 6.1 copy-start
  447.8 6.1 copy-start
  466.2 6.1 copy-start
  484.5 6.1 copy-start
  502.9 6.1 copy-start
  523.8 6.1 copy-start.1
  542.1 6.1 copy-start.1
  560.5 6.1 copy-start.1
  578.8 6.1 copy-start.1
  597.2 6.1 copy-start.1
  615.5 6.1 copy-start.1
Sparse Core Ops, SparseCore 0:
  19.4 50.7 all-gather.1
